TPU v7x, 512 devices: a whole 4x4x16 slice. The times are simulated.
512 devices in a mesh: expert: 8 (over z_hi, x), shard: 64 (over y, z_lo, core).
Axes of the slice: x: 4, y: 4, z: 16 (z_hi: 2, z_lo: 8; z = z_hi * 8 + z_lo), core: 2. Of those that a mesh axis runs over, the one named last changes fastest.
Arguments:
- tokens: bfloat16 [1024, 2048], P('expert', 'shard'), may hold values from -6 to 6
- cotangent: bfloat16 [1024, 2048], P('expert', 'shard'), may hold values from -6 to 6
- expert_ids: int32 [1024, 2], P('expert'), may hold values from 0 to 7, all different within a row; in each aligned block of 128 rows (0 to 127, 128 to 255, ...) at most 48 rows name the same one
- route_weights: float32 [1024, 2], P('expert'), may hold values from 0.2 to 1
- dense_gate: bfloat16 [2048, 11008], P('expert', 'shard'), may hold values from -0.125 to 0.125
- dense_up: bfloat16 [2048, 11008], P('expert', 'shard'), may hold values from -0.125 to 0.125
- dense_down: bfloat16 [11008, 2048], P('shard', 'expert'), may hold values from -0.15625 to 0.15625
- noise_gate: bfloat16 [8, 2048, 1280], P('expert', None, 'shard'), may hold values from -0.125 to 0.125
- noise_up: bfloat16 [8, 2048, 1280], P('expert', None, 'shard'), may hold values from -0.125 to 0.125
- noise_down: bfloat16 [8, 1280, 2048], P('expert', 'shard'), may hold values from -0.0546875 to 0.0546875
Outputs:
- mixed: bfloat16 [1024, 2048], P('expert', 'shard')
- grad_gate: bfloat16 [8, 12288, 2048], P('expert', 'shard')
- grad_up: bfloat16 [8, 12288, 2048], P('expert', 'shard')
- grad_down: bfloat16 [8, 12288, 2048], P('expert', 'shard')
Inputs may be any that keep to these rules, and one draw needn't show every extreme that they name: `expert_ids`: the two experts of a token differ. Within each aligned block of 128 tokens no expert is named by more than 48 tokens, a bound that some block reaches.
All inputs are finite; a program needn't handle non-finite values.
Results may differ from a plain program's by a relative error of at most 0.0058.
Values may be sent and summed in bfloat16 or wider, within the bound.
No kernel may reach another device: no remote copies, remote signals or barrier semaphores. Data moves between devices by JAX's collectives and lax.ppermute only.
A program may use at most 64 MiB of HBM per device.

v0:
```python
import jax
import jax.numpy as jnp
from jax import lax
from jax.sharding import PartitionSpec as P


def local(
    tokens,
    cotangent,
    expert_ids,
    route_weights,
    dense_gate,
    dense_up,
    dense_down,
    noise_gate,
    noise_up,
    noise_down,
):
    experts = lax.axis_size("expert")
    tok_dev = tokens.shape[0]
    capacity = min(tok_dev, 3 * tok_dev // experts)
    rows_total = experts * capacity
    gate_full, up_full = (
        lax.all_gather(dense_gate, "expert", axis=0, tiled=True),
        lax.all_gather(dense_up, "expert", axis=0, tiled=True),
    )
    down_full = lax.all_gather(dense_down, "expert", axis=1, tiled=True)
    wide_gate = jnp.concatenate([gate_full, noise_gate[0]], axis=1)
    wide_up = jnp.concatenate([up_full, noise_up[0]], axis=1)
    wide_down = jnp.concatenate([down_full, noise_down[0]], axis=0)
    pair_ids = expert_ids.reshape(-1)
    onehot = (pair_ids[:, None] == jnp.arange(experts, dtype=jnp.int32)[None, :]).astype(jnp.int32)
    earlier = jnp.cumsum(onehot, axis=0) - onehot
    slot_index = jnp.sum(earlier * onehot, axis=1)
    target = pair_ids * capacity + slot_index
    flat_weights = route_weights.reshape(-1)
    row_width = tokens.shape[1]
    tok_pairs = jnp.repeat(tokens, 2, axis=0)
    cot_pairs = (
        flat_weights[:, None] * jnp.repeat(cotangent, 2, axis=0).astype(jnp.float32)
    ).astype(jnp.bfloat16)
    send_tok = jnp.zeros((rows_total, row_width), jnp.bfloat16).at[target].set(tok_pairs)
    send_cot = jnp.zeros((rows_total, row_width), jnp.bfloat16).at[target].set(cot_pairs)
    send_tok, send_cot = (send_tok, send_cot)
    slot_tok, slot_cot = (
        lax.all_to_all(send_tok, "expert", split_axis=0, concat_axis=0, tiled=True),
        lax.all_to_all(send_cot, "expert", split_axis=0, concat_axis=0, tiled=True),
    )
    inputs, slot_grads = (
        lax.all_gather(slot_tok, "shard", axis=1, tiled=True),
        lax.all_gather(slot_cot, "shard", axis=1, tiled=True),
    )
    gate_pre = jnp.dot(inputs, wide_gate, preferred_element_type=jnp.float32)
    up_pre = jnp.dot(inputs, wide_up, preferred_element_type=jnp.float32)
    sigmoid_gate = jax.nn.sigmoid(gate_pre)
    silu_gate = gate_pre * sigmoid_gate
    hidden = (silu_gate * up_pre).astype(jnp.bfloat16)
    summed = lax.psum_scatter(
        lax.dot_general(
            wide_down, hidden, (((0,), (1,)), ((), ())), preferred_element_type=jnp.float32
        ),
        "shard",
        scatter_dimension=0,
        tiled=True,
    )
    out_slots = summed.astype(jnp.bfloat16)
    returned = lax.all_to_all(out_slots, "expert", split_axis=1, concat_axis=1, tiled=True)
    picked = jnp.take(returned, target, axis=1).astype(jnp.float32)
    weighted = (picked * flat_weights[None, :]).reshape(picked.shape[0], tok_dev, 2)
    mixed = jnp.sum(weighted, axis=2).T.astype(jnp.bfloat16)
    grad_hidden = lax.dot_general(
        slot_grads, wide_down, (((1,), (1,)), ((), ())), preferred_element_type=jnp.float32
    )
    grad_gate_pre = (
        grad_hidden * up_pre * sigmoid_gate * (1.0 + gate_pre * (1.0 - sigmoid_gate))
    ).astype(jnp.bfloat16)
    grad_up_pre = (grad_hidden * silu_gate).astype(jnp.bfloat16)
    contract_rows = (((0,), (0,)), ((), ()))
    grad_gate = lax.dot_general(
        grad_gate_pre, inputs, contract_rows, preferred_element_type=jnp.float32
    ).astype(jnp.bfloat16)
    grad_up = lax.dot_general(
        grad_up_pre, inputs, contract_rows, preferred_element_type=jnp.float32
    ).astype(jnp.bfloat16)
    grad_down = lax.dot_general(
        hidden, slot_grads, contract_rows, preferred_element_type=jnp.float32
    ).astype(jnp.bfloat16)
    return (mixed, grad_gate[None], grad_up[None], grad_down[None])


def solution(mesh):
    in_specs = (
        P("expert", "shard"),
        P("expert", "shard"),
        P("expert", None),
        P("expert", None),
        P("expert", "shard"),
        P("expert", "shard"),
        P("shard", "expert"),
        P("expert", None, "shard"),
        P("expert", None, "shard"),
        P("expert", "shard", None),
    )
    out_specs = (
        P("expert", "shard"),
        P("expert", "shard", None),
        P("expert", "shard", None),
        P("expert", "shard", None),
    )
    return jax.shard_map(local, mesh=mesh, in_specs=in_specs, out_specs=out_specs, check_vma=False)
```

profile of v0, /device:TPU:2, one launch (start us, length us, event | category | flops | bytes accessed | tf_op | source)
XLA Modules:
  0.0 763.7 jit_solution(14176948831567929491)
XLA Ops:
  7.2 0.0 copy-start.4
  7.2 0.0 all-gather.3.cloned.1.call-start
  7.2 0.7 broadcast_multiply_fusion
  7.9 0.8 copy.65
  8.7 0.1 eq.26
  8.8 0.1 reshape.88
  9.0 0.0 copy-start.5
  9.0 0.1 copy.69
  9.1 0.1 mul.65
  9.2 0.6 reduce-window.6
  9.8 0.2 slice_reduce_fusion
  10.1 0.8 copy.70
  10.9 0.1 fusion.22
  11.1 1.2 scatter_custom_fusion
  12.3 0.1 copy.72
  12.4 0.1 reshape.120
  12.5 31.4 %all_to_all.36 = bf16[8,2,768]{2,1,0:T(2,128)(2,1)S(1)} all-to-all(bf16[8,2,768]{2,1,0:T(2,128)(2,1)S(1)} %reshape.120), channel_id=1, replica_groups=mesh['expert'=8,'shard'=64] {'expert'}, dimensions={0} | all-to-all | bytes 49152 | tf_op jit(solution)/shard_map/all_to_all | solution.py:46
  43.9 0.1 reshape.121
  44.0 0.0 copy-start.6
  44.1 0.7 all_to_all.26
  44.8 0.0 all-gather.3.cloned.1.call-update
  44.8 0.0 all-gather.5.cloned.1.call-start
  44.8 0.8 copy.76
  45.6 0.8 copy.78
  46.4 0.1 mul.70
  46.6 1.3 scatter_custom_fusion.1
  47.9 0.1 copy.80
  48.0 0.1 reshape.124
  48.2 17.3 %all_to_all.37 = bf16[8,2,768]{2,1,0:T(2,128)(2,1)S(1)} all-to-all(bf16[8,2,768]{2,1,0:T(2,128)(2,1)S(1)} %reshape.124), channel_id=1, replica_groups=mesh['expert'=8,'shard'=64] {'expert'}, dimensions={0} | all-to-all | bytes 49152 | tf_op jit(solution)/shard_map/all_to_all | solution.py:47
  65.5 0.1 reshape.125
  65.6 0.7 all_to_all.32
  66.4 0.0 all-gather.5.cloned.1.call-update
  66.4 0.0 reduce-scatter.2.cloned.1.call-start
  66.4 0.0 copy-done.4
  66.4 56.7 %all_gather.17 = bf16[2048,172]{0,1:T(8,128)(2,1)} all-gather(bf16[256,172]{0,1:T(8,128)(2,1)S(1)} %copy-done.4), channel_id=1, replica_groups=mesh['expert'=8,'shard'=64] {'expert'}, dimensions={0}, use_global_device_ids=true | all-gather | bytes 792576 | tf_op jit(solution)/shard_map/all_gather | solution.py:24
  123.2 67.1 %all_gather.18 = bf16[2048,172]{0,1:T(8,128)(2,1)S(1)} all-gather(bf16[256,172]{0,1:T(8,128)(2,1)S(1)} %copy-done.5), channel_id=1, replica_groups=mesh['expert'=8,'shard'=64] {'expert'}, dimensions={0}, use_global_device_ids=true | all-gather | bytes 792576 | tf_op jit(solution)/shard_map/all_gather | solution.py:25
  190.3 74.2 %all_gather.15 = bf16[172,2048]{1,0:T(8,128)(2,1)S(1)} all-gather(bf16[172,256]{1,0:T(8,128)(2,1)S(1)} %copy-done.6), channel_id=1, replica_groups=mesh['expert'=8,'shard'=64] {'expert'}, dimensions={1}, use_global_device_ids=true | all-gather | bytes 792576 | tf_op jit(solution)/shard_map/all_gather | solution.py:27
  264.5 2.4 fusion.3
  266.9 0.0 copy-start.3
  266.9 1.3 multiply_convert_fusion.2
  268.2 3.3 fusion.12
  271.6 0.0 reduce-scatter.2.cloned.1.call-update
  271.6 0.1 reduce_sum.23
  271.7 0.1 copy.67
  271.8 0.5 copy-done.7
  272.3 0.1 copy.68
  272.4 11.0 %all-gather.5.cloned.1.call-done = bf16[384,2048]{0,1:T(8,128)(2,1)} async-done(((bf16[384,32]{0,1:T(8,128)(2,1)}), bf16[384,2048]{0,1:T(8,128)(2,1)}) %all-gather.5.cloned.1.call-update) | async-done | bytes 1572880 | tf_op jit(solution)/shard_map/all_gather | solution.py:51
  283.5 2.0 fusion.11
  285.4 0.0 copy-start.2
  285.4 1.6 fusion.1
  287.1 0.0 copy-done.2
  287.1 1.6 fusion
  288.7 442.6 %reduce-scatter.2.cloned.1.call-done = f32[32,384]{1,0:T(8,128)} async-done(((f32[2048,384]{1,0:T(8,128)}), f32[32,384]{1,0:T(8,128)}) %reduce-scatter.2.cloned.1.call-update) | async-done | bytes 49168 | tf_op jit(solution)/shard_map/reduce_scatter | solution.py:58
  731.2 0.8 convert_element_type.51
  732.0 0.1 all_to_all.27
  732.2 0.7 reshape.122
  732.9 8.6 %all-to-all-start.1 = ((bf16[8,2,768]{2,1,0:T(2,128)(2,1)}), bf16[8,2,768]{2,1,0:T(2,128)(2,1)S(1)}, u32[]{:S(2)}, u32[]{:S(2)}) async-start(bf16[8,2,768]{2,1,0:T(2,128)(2,1)} %reshape.122), calls=%async_computation.2 | async-start | bytes 49152 | tf_op jit(solution)/shard_map/all_to_all | solution.py:67
  741.5 2.5 fusion.2
  744.0 11.0 %all-to-all-done.1 = bf16[8,2,768]{2,1,0:T(2,128)(2,1)S(1)} async-done(((bf16[8,2,768]{2,1,0:T(2,128)(2,1)}), bf16[8,2,768]{2,1,0:T(2,128)(2,1)S(1)}, u32[]{:S(2)}, u32[]{:S(2)}) %all-to-all-start.1) | async-done | bytes 24608 | tf_op jit(solution)/shard_map/all_to_all | solution.py:67
  755.0 0.1 reshape.123
  755.1 0.1 copy.75
  755.3 0.9 gather_fusion
  756.1 0.4 multiply_reduce_fusion
  756.5 0.7 copy.82
  (22 shorter events, 0.2 us)
Async XLA Ops:
  7.2 59.3 %copy-start.4 = (bf16[256,172]{0,1:T(8,128)(2,1)S(1)}, bf16[256,172]{0,1:T(8,128)(2,1)}, u32[]{:S(2)}) copy-start(bf16[256,172]{0,1:T(8,128)(2,1)} %param.14) | copy-start | bytes 264196
  7.2 257.3 %all-gather.3.cloned.1.call-start = ((), (), s32[]{:S(2)}) async-start(), calls=%async_computation.4 | async-start | bytes 1597440 | tf_op jit(solution)/shard_map/all_gather | solution.py:50
  9.0 114.2 %copy-start.5 = (bf16[256,172]{0,1:T(8,128)(2,1)S(1)}, bf16[256,172]{0,1:T(8,128)(2,1)}, u32[]{:S(2)}) copy-start(bf16[256,172]{0,1:T(8,128)(2,1)} %param.15) | copy-start | bytes 264196
  44.0 146.3 %copy-start.6 = (bf16[172,256]{1,0:T(8,128)(2,1)S(1)}, bf16[172,256]{1,0:T(8,128)(2,1)}, u32[]{:S(2)}) copy-start(bf16[172,256]{1,0:T(8,128)(2,1)} %param.16) | copy-start | bytes 264196
  44.8 238.7 %all-gather.5.cloned.1.call-start = ((), (), s32[]{:S(2)}) async-start(), calls=%async_computation.6 | async-start | bytes 1597440 | tf_op jit(solution)/shard_map/all_gather | solution.py:51
  66.4 664.8 %reduce-scatter.2.cloned.1.call-start = ((), (), s32[]{:S(2)}) async-start(), calls=%async_computation.5 | async-start | bytes 3194880 | tf_op jit(solution)/shard_map/reduce_scatter | solution.py:58
  264.5 2.4 copy-start
  264.5 2.4 copy-start.8
  266.9 1.4 copy-start.3
  271.6 0.7 copy-start.7
  285.4 1.6 copy-start.2
  287.1 454.5 %copy-start.1 = (bf16[384,2048]{0,1:T(8,128)(2,1)S(1)}, bf16[384,2048]{0,1:T(8,128)(2,1)}, u32[]{:S(2)}) copy-start(bf16[384,2048]{0,1:T(8,128)(2,1)} %all-gather.5.cloned.1.call-done) | copy-start | bytes 4718596
  732.9 22.1 %all-to-all-start.1 = ((bf16[8,2,768]{2,1,0:T(2,128)(2,1)}), bf16[8,2,768]{2,1,0:T(2,128)(2,1)S(1)}, u32[]{:S(2)}, u32[]{:S(2)}) async-start(bf16[8,2,768]{2,1,0:T(2,128)(2,1)} %reshape.122), calls=%async_computation.2 | async-start | bytes 49152 | tf_op jit(solution)/shard_map/all_to_all | solution.py:67
Sparse Core Ops, SparseCore 0:
  44.9 113.7 all-gather.2
  161.5 121.9 all-gather.4
  286.3 444.9 reduce-scatter.1
where the time goes:
time: 764 us
  waiting for transfers between devices  465 us (61%)
  blocking collectives  247 us (32%)
  matrix products  14.7 us (2%)
  between operations  14 us (2%)
  local copies, waits for them, and re-layouts  11 us (1%)
  starting transfers between devices  8.76 us (1%)
    reduce_scatter x1, waiting for transfers between devices, local(): lax.psum_scatter(lax.dot_general(wide_down, hidden, (((0,), (1,)), ((), (...  443 us
    all_gather x1, blocking collectives, local(): down_full = lax.all_gather(dense_down, 'expert', axis=1, tiled=True)  74.2 us
    all_gather x1, blocking collectives, local(): lax.all_gather(dense_up, 'expert', axis=0, tiled=True)  67.1 us
    all_gather x1, blocking collectives, local(): lax.all_gather(dense_gate, 'expert', axis=0, tiled=True)  56.7 us
    all_to_all x1, blocking collectives, local(): lax.all_to_all(send_tok, 'expert', split_axis=0, concat_axis=0, tiled=True)  31.4 us
    all_to_all x1, blocking collectives, local(): lax.all_to_all(send_cot, 'expert', split_axis=0, concat_axis=0, tiled=True)  17.3 us
  transfers between devices with their start and end apart: 4, of which 3 were waited for; matrix products, arithmetic and copies ran while one was open for 2% of the time, Pallas kernels for 0%

commit v1 on v0

--- a/solution.py
+++ b/solution.py
@@ -22,7 +22,15 @@
     rows_total = experts * capacity
     gate_full, up_full = (
         lax.all_gather(dense_gate, "expert", axis=0, tiled=True),
-        lax.all_gather(dense_up, "expert", axis=0, tiled=True),
+        jnp.concatenate(
+            lax.all_to_all(
+                jnp.stack([dense_up for _ in range(lax.psum(1, axis_name="expert"))], axis=0),
+                concat_axis=0,
+                split_axis=0,
+                axis_name="expert",
+            ),
+            0,
+        ),
     )
     down_full = lax.all_gather(dense_down, "expert", axis=1, tiled=True)
     wide_gate = jnp.concatenate([gate_full, noise_gate[0]], axis=1)

time: 764 us -> 797 us (1.043)
  waiting for transfers between devices: 465 us -> 526 us
  blocking collectives: 247 us -> 213 us
    all_gather x1, waiting for transfers between devices: 11 us -> 80.7 us  [local(): lax.all_gather(slot_cot, 'shard', axis=1, tiled=True)]
    all_gather x1 -> x0, blocking collectives: 67.1 us -> none  [local(): lax.all_gather(dense_up, 'expert', axis=0, tiled=True)]
    all_gather x1, blocking collectives: 56.7 us -> 84.1 us  [local(): lax.all_gather(dense_gate, 'expert', axis=0, tiled=True)]
  transfers between devices with their start and end apart: 4 -> 5, of which waited for: 3 -> 3; matrix products, arithmetic and copies ran while one was open for 2% -> 2% of each run, Pallas kernels for 0% -> 0%
where the time goes in v1:
time: 797 us; the launch traced here: 796 us
  waiting for transfers between devices  526 us (66%)
  blocking collectives  213 us (27%)
  between operations  14 us (2%)
  local copies, waits for them, and re-layouts  13.5 us (2%)
  matrix products  13.3 us (2%)
  starting transfers between devices  12.8 us (2%)
    reduce_scatter x1, waiting for transfers between devices, local(): lax.psum_scatter(lax.dot_general(wide_down, hidden, (((0,), (1,)), ((), (...  435 us
    all_gather x1, blocking collectives, local(): lax.all_gather(dense_gate, 'expert', axis=0, tiled=True)  84.1 us
    all_gather x1, waiting for transfers between devices, local(): lax.all_gather(slot_cot, 'shard', axis=1, tiled=True)  80.7 us
    all_gather x1, blocking collectives, local(): down_full = lax.all_gather(dense_down, 'expert', axis=1, tiled=True)  79.9 us
    all_to_all x1, blocking collectives, local(): lax.all_to_all(send_tok, 'expert', split_axis=0, concat_axis=0, tiled=True)  31.4 us
    all_to_all x1, blocking collectives, local(): lax.all_to_all(send_cot, 'expert', split_axis=0, concat_axis=0, tiled=True)  17.3 us
  transfers between devices with their start and end apart: 5, of which 3 were waited for; matrix products, arithmetic and copies ran while one was open for 2% of the time, Pallas kernels for 0%

profile of v1, /device:TPU:2, one launch (start us, length us, event | category | flops | bytes accessed | tf_op | source)
XLA Modules:
  0.0 796.1 jit_solution(16748841665362500584)
XLA Ops:
  7.2 0.0 all-gather.3.cloned.1.call-start
  7.2 0.7 broadcast_multiply_fusion
  7.9 0.8 copy.72
  8.7 0.1 eq.26
  8.8 0.1 reshape.93
  9.0 0.1 copy.76
  9.1 0.1 mul.65
  9.2 0.6 reduce-window.6
  9.8 0.2 slice_reduce_fusion
  10.1 0.8 copy.77
  10.9 0.1 fusion.22
  11.0 1.2 scatter_custom_fusion
  12.3 0.1 copy.79
  12.4 0.1 reshape.126
  12.5 31.4 %all_to_all.41 = bf16[8,2,768]{2,1,0:T(2,128)(2,1)S(1)} all-to-all(bf16[8,2,768]{2,1,0:T(2,128)(2,1)S(1)} %reshape.126), channel_id=1, replica_groups=mesh['expert'=8,'shard'=64] {'expert'}, dimensions={0} | all-to-all | bytes 49152 | tf_op jit(solution)/shard_map/all_to_all | solution.py:54
  43.9 0.1 reshape.127
  44.0 0.7 all_to_all.29
  44.7 0.0 all-gather.3.cloned.1.call-update
  44.8 0.8 copy.84
  45.6 0.8 copy.86
  46.4 0.1 mul.70
  46.5 0.0 copy-start.4
  46.6 1.3 scatter_custom_fusion.1
  47.9 0.1 copy.88
  48.0 0.1 reshape.130
  48.1 17.3 %all_to_all.42 = bf16[8,2,768]{2,1,0:T(2,128)(2,1)S(1)} all-to-all(bf16[8,2,768]{2,1,0:T(2,128)(2,1)S(1)} %reshape.130), channel_id=1, replica_groups=mesh['expert'=8,'shard'=64] {'expert'}, dimensions={0} | all-to-all | bytes 49152 | tf_op jit(solution)/shard_map/all_to_all | solution.py:55
  65.4 0.9 stack.2
  66.3 4.9 all-to-all-start.1
  71.2 0.1 reshape.131
  71.4 0.7 all_to_all.36
  72.1 0.0 all-gather.5.cloned.1.call-update
  72.1 0.0 reduce-scatter.2.cloned.1.call-start
  72.2 84.1 %all_gather.14 = bf16[2048,172]{0,1:T(8,128)(2,1)S(1)} all-gather(bf16[256,172]{0,1:T(8,128)(2,1)S(1)} %copy-done.4), channel_id=1, replica_groups=mesh['expert'=8,'shard'=64] {'expert'}, dimensions={0}, use_global_device_ids=true | all-gather | bytes 792576 | tf_op jit(solution)/shard_map/all_gather | solution.py:24
  156.3 79.9 %all_gather.12 = bf16[172,2048]{1,0:T(8,128)(2,1)S(1)} all-gather(bf16[172,256]{1,0:T(8,128)(2,1)S(1)} %copy-done.5), channel_id=1, replica_groups=mesh['expert'=8,'shard'=64] {'expert'}, dimensions={1}, use_global_device_ids=true | all-gather | bytes 792576 | tf_op jit(solution)/shard_map/all_gather | solution.py:35
  236.2 0.0 all-to-all-done.1
  236.2 0.2 copy.98
  236.4 0.0 copy-start.7
  236.5 1.0 copy.95
  237.6 2.1 fusion.3
  239.7 0.0 copy-start.2
  239.7 0.6 multiply_convert_fusion.2
  240.3 0.3 copy-done.2
  240.6 2.4 fusion.12
  243.0 0.0 reduce-scatter.2.cloned.1.call-update
  243.0 0.1 reduce_sum.23
  243.2 0.1 copy.74
  243.2 0.5 copy-done.6
  243.7 0.1 copy.75
  243.9 80.7 %all-gather.5.cloned.1.call-done = bf16[384,2048]{0,1:T(8,128)(2,1)} async-done(((bf16[384,32]{0,1:T(8,128)(2,1)}), bf16[384,2048]{0,1:T(8,128)(2,1)}) %all-gather.5.cloned.1.call-update) | async-done | bytes 1572880 | tf_op jit(solution)/shard_map/all_gather | solution.py:59
  324.5 2.0 fusion.11
  326.5 1.6 fusion.1
  328.1 1.6 fusion
  329.7 434.7 %reduce-scatter.2.cloned.1.call-done = f32[32,384]{1,0:T(8,128)} async-done(((f32[2048,384]{1,0:T(8,128)}), f32[32,384]{1,0:T(8,128)}) %reduce-scatter.2.cloned.1.call-update) | async-done | bytes 49168 | tf_op jit(solution)/shard_map/reduce_scatter | solution.py:66
  764.5 0.8 convert_element_type.51
  765.3 0.1 all_to_all.31
  765.4 0.7 reshape.128
  766.1 7.8 all-to-all-start.2
  773.9 3.0 fusion.2
  776.9 10.5 %all-to-all-done.2 = bf16[8,2,768]{2,1,0:T(2,128)(2,1)S(1)} async-done(((bf16[8,2,768]{2,1,0:T(2,128)(2,1)}), bf16[8,2,768]{2,1,0:T(2,128)(2,1)S(1)}, u32[]{:S(2)}, u32[]{:S(2)}) %all-to-all-start.2) | async-done | bytes 24608 | tf_op jit(solution)/shard_map/all_to_all | solution.py:75
  787.4 0.1 reshape.129
  787.5 0.1 copy.83
  787.6 0.9 gather_fusion
  788.5 0.4 multiply_reduce_fusion
  788.9 0.7 copy.90
  (27 shorter events, 0.3 us)
Async XLA Ops:
  7.2 58.3 %copy-start.3 = (bf16[256,172]{0,1:T(8,128)(2,1)S(1)}, bf16[256,172]{0,1:T(8,128)(2,1)}, u32[]{:S(2)}) copy-start(bf16[256,172]{0,1:T(8,128)(2,1)} %param.15) | copy-start | bytes 264196
  7.2 230.4 %all-gather.3.cloned.1.call-start = ((), (), s32[]{:S(2)}) async-start(), calls=%async_computation.5 | async-start | bytes 1597440 | tf_op jit(solution)/shard_map/all_gather | solution.py:58
  46.5 25.6 %copy-start.4 = (bf16[256,172]{0,1:T(8,128)(2,1)S(1)}, bf16[256,172]{0,1:T(8,128)(2,1)}, u32[]{:S(2)}) copy-start(bf16[256,172]{0,1:T(8,128)(2,1)} %param.14) | copy-start | bytes 264196
  65.4 90.8 %copy-start.5 = (bf16[172,256]{1,0:T(8,128)(2,1)S(1)}, bf16[172,256]{1,0:T(8,128)(2,1)}, u32[]{:S(2)}) copy-start(bf16[172,256]{1,0:T(8,128)(2,1)} %param.16) | copy-start | bytes 264196
  66.3 169.9 %all-to-all-start.1 = ((bf16[8,256,172]{1,2,0:T(8,128)(2,1)}), bf16[8,256,172]{1,2,0:T(8,128)(2,1)S(1)}, u32[]{:S(2)}, u32[]{:S(2)}) async-start(bf16[8,256,172]{1,2,0:T(8,128)(2,1)} %stack.2), calls=%async_computation.1 | async-start | bytes 1441792 | tf_op jit(solution)/shard_map/all_to_all | solution.py:26
  71.2 253.3 %all-gather.5.cloned.1.call-start = ((), (), s32[]{:S(2)}) async-start(), calls=%async_computation.7 | async-start | bytes 1597440 | tf_op jit(solution)/shard_map/all_gather | solution.py:59
  72.1 692.3 %reduce-scatter.2.cloned.1.call-start = ((), (), s32[]{:S(2)}) async-start(), calls=%async_computation.6 | async-start | bytes 3194880 | tf_op jit(solution)/shard_map/reduce_scatter | solution.py:66
  236.4 1.1 copy-start.7
  237.5 2.1 copy-start
  237.5 2.2 copy-start.1
  237.5 2.2 copy-start.8
  239.7 0.9 copy-start.2
  243.0 0.7 copy-start.6
  766.1 21.3 %all-to-all-start.2 = ((bf16[8,2,768]{2,1,0:T(2,128)(2,1)}), bf16[8,2,768]{2,1,0:T(2,128)(2,1)S(1)}, u32[]{:S(2)}, u32[]{:S(2)}) async-start(bf16[8,2,768]{2,1,0:T(2,128)(2,1)} %reshape.128), calls=%async_computation.3 | async-start | bytes 49152 | tf_op jit(solution)/shard_map/all_to_all | solution.py:75
Sparse Core Ops, SparseCore 0:
  44.9 142.0 all-gather.2
  189.8 134.7 all-gather.4
  327.3 437.0 reduce-scatter.1
